TPU v7x, 32 devices: a whole 2x2x4 slice. The times are simulated.
32 devices in a mesh: seq: 8 (over y, x, core), head: 4 (over z).
Axes of the slice: x: 2, y: 2, z: 4, core: 2. Of those that a mesh axis runs over, the one named last changes fastest.
Arguments:
- query: bfloat16 [2048, 4096], P('seq', 'head'), may hold values from -6 to 6
- key: bfloat16 [2048, 4096], P('seq', 'head'), may hold values from -6 to 6
- value: bfloat16 [2048, 4096], P('seq', 'head'), may hold values from -6 to 6
- head_gain: float32 [4096], P('head'), may hold values from 0.1 to 1.9
- out_weight: bfloat16 [4096, 4096], P('head', 'seq'), may hold values from -0.09375 to 0.09375
- stream: bfloat16 [2048, 4096], P(('seq', 'head')), may hold values from -6 to 6
- model_gain: float32 [4096], replicated, may hold values from 0.1 to 1.9
- expert_ids: int32 [2048, 8], P(('seq', 'head')), may hold values from 0 to 31, all different within a row; in each aligned block of 64 rows (0 to 63, 64 to 127, ...) at most 24 rows name the same one
- expert_gates: float32 [2048, 8], P(('seq', 'head')), may hold values from 0.1 to 0.5
- gate_weight: bfloat16 [32, 4096, 768], P(('seq', 'head')), may hold values from -0.09375 to 0.09375
- up_weight: bfloat16 [32, 4096, 768], P(('seq', 'head')), may hold values from -0.09375 to 0.09375
- down_weight: bfloat16 [32, 768, 4096], P(('seq', 'head')), may hold values from -0.21875 to 0.21875
- weight_scales: float32 [32, 3], P(('seq', 'head')), may hold values from 0.6 to 1.6
Outputs:
- layer_out: bfloat16 [2048, 4096], P(('seq', 'head'))
Inputs may be any that keep to these rules, and one draw needn't show every extreme that they name: `expert_ids`: among the 64 tokens of one device (aligned blocks of rows), no expert is named more than 24 times, a bound that some block reaches; the entries of one row differ.
All inputs are finite; a program needn't handle non-finite values.
Results may differ from a plain program's by a relative error of at most 0.013.
Values may be sent and summed in bfloat16 or wider, within the bound.
A program may use at most 128 MiB of HBM per device.

v0:
```python
import jax
import jax.numpy as jnp
from jax import lax
from jax.sharding import PartitionSpec as P

D = 4096
HD = 128
TOPK = 8


def body(
    query,
    key,
    value,
    head_gain,
    out_weight,
    stream,
    model_gain,
    expert_ids,
    expert_gates,
    gate_weight,
    up_weight,
    down_weight,
    weight_scales,
):
    seq_rows = query.shape[0]
    heads_local = head_gain.shape[0] // HD
    query_rows = query.reshape(seq_rows, heads_local, HD)
    key_rows = key.reshape(seq_rows, heads_local, HD)
    value_rows = value.reshape(seq_rows, heads_local, HD)
    scores = jnp.einsum("thd,shd->hts", query_rows, key_rows, preferred_element_type=jnp.float32)
    causal = jnp.tril(jnp.ones((seq_rows, seq_rows), dtype=bool))
    scores = jnp.where(causal[None, :, :], scores, 0.0).astype(jnp.bfloat16)
    local_part = jnp.einsum("hts,shd->thd", scores, value_rows, preferred_element_type=jnp.float32)
    block_state = jnp.einsum(
        "shd,she->hde", key_rows, value_rows, preferred_element_type=jnp.float32
    )
    position = lax.axis_index("seq")
    pieces = lax.all_gather(block_state[None], "seq", axis=0, tiled=True)
    piece_count = pieces.shape[0]
    selected = (jnp.arange(piece_count, dtype=jnp.int32) < position).astype(jnp.float32)
    prior_state = jnp.einsum("n,nhde->hde", selected, pieces)
    earlier_part = jnp.einsum(
        "thd,hde->the",
        query_rows,
        prior_state.astype(jnp.bfloat16),
        preferred_element_type=jnp.float32,
    )
    mixed_heads = local_part + earlier_part
    mean_square = jnp.mean(mixed_heads * mixed_heads, axis=-1, keepdims=True)
    head_normed = (
        mixed_heads * lax.rsqrt(mean_square + 1e-06) * head_gain.reshape(heads_local, HD)
    ).astype(jnp.bfloat16)
    head_normed = head_normed.reshape(seq_rows, heads_local * HD)
    full_out = lax.all_gather(out_weight, "seq", axis=1, tiled=True)
    tok_rows = stream.shape[0]
    attention = lax.psum_scatter(
        jnp.dot(head_normed, full_out, preferred_element_type=jnp.float32),
        "head",
        scatter_dimension=0,
        tiled=True,
    )
    residual_float = (
        (stream.astype(jnp.float32) + attention).astype(jnp.bfloat16).astype(jnp.float32)
    )
    mean_square = jnp.mean(residual_float * residual_float, axis=-1, keepdims=True)
    normed = (residual_float * lax.rsqrt(mean_square + 1e-06) * model_gain).astype(jnp.bfloat16)
    seq_count = lax.axis_size("seq")
    head_count = lax.axis_size("head")
    experts = seq_count * head_count
    capacity = 3 * tok_rows * TOPK // (2 * experts)
    flat_ids = expert_ids.reshape(-1)
    onehot = (flat_ids[:, None] == jnp.arange(experts, dtype=jnp.int32)[None, :]).astype(jnp.int32)
    earlier_count = jnp.cumsum(onehot, axis=0) - onehot
    slot_index = jnp.sum(earlier_count * onehot, axis=1)
    target = flat_ids * capacity + slot_index
    source_rows = jnp.broadcast_to(normed[:, None, :], (tok_rows, TOPK, D)).reshape(
        tok_rows * TOPK, D
    )
    outgoing = jnp.zeros((experts * capacity, D), jnp.bfloat16).at[target].set(source_rows)
    outgoing = outgoing.reshape(experts, capacity, D)
    scale_row = weight_scales[0]
    slot_rows = lax.all_to_all(outgoing, ("seq", "head"), split_axis=0, concat_axis=0, tiled=True)
    gate_part = (
        jnp.einsum("smd,df->smf", slot_rows, gate_weight[0], preferred_element_type=jnp.float32)
        * scale_row[0]
    )
    up_part = (
        jnp.einsum("smd,df->smf", slot_rows, up_weight[0], preferred_element_type=jnp.float32)
        * scale_row[1]
    )
    act = (jax.nn.silu(gate_part) * up_part).astype(jnp.bfloat16)
    produced = (
        jnp.einsum("smf,fd->smd", act, down_weight[0], preferred_element_type=jnp.float32)
        * scale_row[2]
    )
    computed = produced.astype(jnp.bfloat16)
    results = lax.all_to_all(computed, ("seq", "head"), split_axis=0, concat_axis=0, tiled=True)
    gathered = results.reshape(experts * capacity, D)[target].reshape(tok_rows, TOPK, D)
    expert_mix = jnp.sum(gathered.astype(jnp.float32) * expert_gates[:, :, None], axis=1)
    return (residual_float + expert_mix).astype(jnp.bfloat16)


def solution(mesh):
    return jax.shard_map(
        body,
        mesh=mesh,
        in_specs=(
            P("seq", "head"),
            P("seq", "head"),
            P("seq", "head"),
            P("head"),
            P("head", "seq"),
            P(("seq", "head"), None),
            P(),
            P(("seq", "head"), None),
            P(("seq", "head"), None),
            P(("seq", "head"), None, None),
            P(("seq", "head"), None, None),
            P(("seq", "head"), None, None),
            P(("seq", "head"), None),
        ),
        out_specs=P(("seq", "head"), None),
        check_vma=False,
    )
```

profile of v0, /device:TPU:25, one launch (start us, length us, event | category | flops | bytes accessed | tf_op | source)
XLA Modules:
  0.0 528.4 jit_solution(8863378836892330042)
XLA Ops:
  6.5 1.3 copy.42
  7.9 2.1 fusion.24
  10.0 0.7 all-gather.4.cloned.1.call-update
  10.8 28.5 %all-gather.6.cloned.1.call-done = bf16[64,128,128]{2,1,0:T(8,128)(2,1)} async-done(((bf16[8,128,128]{2,1,0:T(8,128)(2,1)}), bf16[64,128,128]{2,1,0:T(8,128)(2,1)}) %all-gather.6.cloned.1.call-update) | async-done | bytes 2097168 | tf_op jit(solution)/shard_map/all_gather | solution.py:39
  39.3 3.0 fusion.8
  43.0 1.8 multiply_reduce_fusion
  44.8 1.4 multiply_convert_fusion.2
  46.2 50.8 %all-gather.4.cloned.1.call-done = bf16[1024,4096]{1,0:T(8,128)(2,1)} async-done(((bf16[1024,512]{1,0:T(8,128)(2,1)}), bf16[1024,4096]{1,0:T(8,128)(2,1)}) %all-gather.4.cloned.1.call-update) | async-done | bytes 8388624 | tf_op jit(solution)/shard_map/all_gather | solution.py:55
  97.1 7.7 %fusion.46 = f32[256,4096]{1,0:T(8,128)} fusion(bf16[256,1024]{0,1:T(8,128)(2,1)S(1)} %bitcast.102, bf16[1024,4096]{1,0:T(8,128)(2,1)} %all-gather.4.cloned.1.call-done), kind=kOutput, calls=%fused_computation.65 | convolution fusion | flops 2147483648 | bytes 13107200 | tf_op jit(solution)/shard_map/dot_general | solution.py:58
  104.8 0.7 copy-done.5
  105.8 1.2 reduce-window.6
  107.5 73.3 %reduce-scatter.2.cloned.1.call-done = f32[64,4096]{1,0:T(8,128)} async-done(((f32[256,4096]{1,0:T(8,128)}), f32[64,4096]{1,0:T(8,128)}) %reduce-scatter.2.cloned.1.call-update) | async-done | bytes 1048592 | tf_op jit(solution)/shard_map/reduce_scatter | solution.py:57
  180.8 1.5 fusion.17
  182.5 9.8 %scatter_custom_fusion = bf16[768,4096]{1,0:T(8,128)(2,1)} fusion(s32[512]{0:T(512)S(1)} %bitcast.106, bf16[]{:T(256)} %constant.10.clone.1, bf16[64,4096]{1,0:T(8,128)(2,1)S(1)} %fusion.19), kind=kCustom, calls=%fused_computation.10 | custom fusion | bytes 6815746 | tf_op jit(solution)/shard_map/scatter | solution.py:80
  192.3 6.3 %all-to-all-start = ((bf16[32,24,4096]{2,1,0:T(8,128)(2,1)}), bf16[32,24,4096]{2,1,0:T(8,128)(2,1)}, u32[]{:S(2)}, u32[]{:S(2)}) async-start(bf16[32,24,4096]{2,1,0:T(8,128)(2,1)} %bitcast.101), calls=%async_computation.1 | async-start | bytes 12582912 | tf_op jit(solution)/shard_map/all_to_all | solution.py:83
  199.2 132.2 %all-to-all-done = bf16[32,24,4096]{2,1,0:T(8,128)(2,1)} async-done(((bf16[32,24,4096]{2,1,0:T(8,128)(2,1)}), bf16[32,24,4096]{2,1,0:T(8,128)(2,1)}, u32[]{:S(2)}, u32[]{:S(2)}) %all-to-all-start) | async-done | bytes 6291488 | tf_op jit(solution)/shard_map/all_to_all | solution.py:83
  331.4 9.2 %fusion.2 = f32[32,24,768]{2,1,0:T(8,128)S(1)} fusion(bf16[32,24,4096]{2,1,0:T(8,128)(2,1)} %all-to-all-done, bf16[1,4096,768]{2,1,0:T(8,128)(2,1)} %param.23), kind=kOutput, calls=%fused_computation.6 | convolution fusion | flops 4831838208 | bytes 14942208 | tf_op jit(solution)/shard_map/smd,df->smf/dot_general | solution.py:89
  340.6 10.7 %multiply_convert_fusion.1 = bf16[32,24,768]{2,1,0:T(8,128)(2,1)S(1)} fusion(f32[32,24,768]{2,1,0:T(8,128)S(1)} %fusion.2, bf16[32,24,4096]{2,1,0:T(8,128)(2,1)} %all-to-all-done, bf16[1,4096,768]{2,1,0:T(8,128)(2,1)} %param.22, f32[]{:T(128)} %bitcast.18, f32[]{:T(128)} %bitcast.15), kind=kOutput, calls=%fused_computation.15 | convolution fusion | flops 4836556800 | bytes 16121864 | tf_op jit(solution)/shard_map/smd,df->smf/dot_general | solution.py:85
  351.4 7.7 %multiply_convert_fusion = bf16[32,24,4096]{2,1,0:T(8,128)(2,1)} fusion(bf16[32,24,768]{2,1,0:T(8,128)(2,1)S(1)} %multiply_convert_fusion.1, bf16[1,768,4096]{2,1,0:T(8,128)(2,1)S(1)} %bitcast.111, f32[]{:T(128)} %bitcast.21), kind=kOutput, calls=%fused_computation.2 | convolution fusion | flops 4838129664 | bytes 13762564 | tf_op jit(solution)/shard_map/smf,fd->smd/dot_general | solution.py:94
  359.1 11.0 %all-to-all-start.1 = ((bf16[32,24,4096]{2,1,0:T(8,128)(2,1)}), bf16[32,24,4096]{2,1,0:T(8,128)(2,1)}, u32[]{:S(2)}, u32[]{:S(2)}) async-start(bf16[32,24,4096]{2,1,0:T(8,128)(2,1)} %multiply_convert_fusion), calls=%async_computation.2 | async-start | bytes 12582912 | tf_op jit(solution)/shard_map/all_to_all | solution.py:98
  370.2 132.8 %all-to-all-done.1 = bf16[32,24,4096]{2,1,0:T(8,128)(2,1)} async-done(((bf16[32,24,4096]{2,1,0:T(8,128)(2,1)}), bf16[32,24,4096]{2,1,0:T(8,128)(2,1)}, u32[]{:S(2)}, u32[]{:S(2)}) %all-to-all-start.1) | async-done | bytes 6291488 | tf_op jit(solution)/shard_map/all_to_all | solution.py:98
  503.0 12.3 %gather_fusion = bf16[512,4096]{1,0:T(8,128)(2,1)} fusion(bf16[768,4096]{1,0:T(8,128)(2,1)} %bitcast.22, s32[1024]{0:T(1024)S(1)} %pad_clamp_fusion), kind=kCustom, calls=%fused_computation | custom fusion | bytes 8390656 | tf_op jit(solution)/shard_map/gather | solution.py:99
  515.2 5.7 %fusion = f32[64,4096]{1,0:T(8,128)S(1)} fusion(bf16[512,4096]{1,0:T(8,128)(2,1)} %gather_fusion, f32[64,8]{1,0:T(8,128)S(1)} %copy.38), kind=kLoop, calls=%fused_computation.4 | loop fusion | flops 6029312 | bytes 5244928 | tf_op jit(solution)/shard_map/reduce_sum | solution.py:100
  520.9 0.9 fusion.20
  (48 shorter events, 2.6 us)
Async XLA Ops:
  6.5 36.2 %copy-start = (bf16[256,1024]{1,0:T(8,128)(2,1)S(1)}, bf16[256,1024]{1,0:T(8,128)(2,1)}, u32[]{:S(2)}) copy-start(bf16[256,1024]{1,0:T(8,128)(2,1)} %param.13) | copy-start | bytes 1572868
  6.5 32.7 %all-gather.6.cloned.1.call-start = ((), (), s32[]{:S(2)}) async-start(), calls=%async_computation.5 | async-start | bytes 2359296 | tf_op jit(solution)/shard_map/all_gather | solution.py:39
  7.8 35.2 %copy-start.3 = (bf16[256,1024]{1,0:T(8,128)(2,1)S(1)}, bf16[256,1024]{1,0:T(8,128)(2,1)}, u32[]{:S(2)}) copy-start(bf16[256,1024]{1,0:T(8,128)(2,1)} %param.15) | copy-start | bytes 1572868
  10.0 87.1 %all-gather.4.cloned.1.call-start = ((), (), s32[]{:S(2)}) async-start(), calls=%async_computation.3 | async-start | bytes 9437184 | tf_op jit(solution)/shard_map/all_gather | solution.py:55
  10.7 170.1 %reduce-scatter.2.cloned.1.call-start = ((), (), s32[]{:S(2)}) async-start(), calls=%async_computation.4 | async-start | bytes 5242880 | tf_op jit(solution)/shard_map/reduce_scatter | solution.py:57
  39.3 5.5 %copy-start.7 = (f32[1024]{0:T(1024)S(1)}, f32[1024]{0:T(1024)}, u32[]{:S(2)}) copy-start(f32[1024]{0:T(1024)} %param.16) | copy-start | bytes 12292
  104.8 0.7 copy-start.5
  104.8 76.0 %copy-start.2 = (bf16[64,4096]{1,0:T(8,128)(2,1)S(1)}, bf16[64,4096]{1,0:T(8,128)(2,1)}, u32[]{:S(2)}) copy-start(bf16[64,4096]{1,0:T(8,128)(2,1)} %param.18) | copy-start | bytes 1572868
  104.8 77.5 %copy-start.4 = (f32[4096]{0:T(1024)S(1)}, f32[4096]{0:T(1024)}, u32[]{:S(2)}) copy-start(f32[4096]{0:T(1024)} %param.19) | copy-start | bytes 49156
  192.3 6.4 %copy-start.6 = (f32[1,3]{1,0:T(1,128)S(1)}, f32[1,3]{1,0:T(1,128)}, u32[]{:S(2)}) copy-start(f32[1,3]{1,0:T(1,128)} %param.25) | copy-start | bytes 40
  192.3 139.2 %all-to-all-start = ((bf16[32,24,4096]{2,1,0:T(8,128)(2,1)}), bf16[32,24,4096]{2,1,0:T(8,128)(2,1)}, u32[]{:S(2)}, u32[]{:S(2)}) async-start(bf16[32,24,4096]{2,1,0:T(8,128)(2,1)} %bitcast.101), calls=%async_computation.1 | async-start | bytes 12582912 | tf_op jit(solution)/shard_map/all_to_all | solution.py:83
  331.4 19.9 %slice-start = ((s8[6291456]{0:T(1024)(128)(4,1)}), s8[4194304]{0:T(1024)(128)(4,1)S(1)}, s32[]{:S(2)}) async-start(s8[6291456]{0:T(1024)(128)(4,1)} %bitcast.110), calls=%async_computation.6 | async-start | bytes 8388608
  340.6 10.8 %slice-start.1 = ((s8[6291456]{0:T(1024)(128)(4,1)}), s8[2097152]{0:T(1024)(128)(4,1)S(1)}, s32[]{:S(2)}) async-start(s8[6291456]{0:T(1024)(128)(4,1)} %bitcast.110), calls=%async_computation.7 | async-start | bytes 4194304
  359.1 11.0 %copy-start.8 = (f32[64,8]{0,1:T(8,128)S(1)}, f32[64,8]{0,1:T(8,128)}, u32[]{:S(2)}) copy-start(f32[64,8]{0,1:T(8,128)} %param.21) | copy-start | bytes 6148
  359.1 143.9 %all-to-all-start.1 = ((bf16[32,24,4096]{2,1,0:T(8,128)(2,1)}), bf16[32,24,4096]{2,1,0:T(8,128)(2,1)}, u32[]{:S(2)}, u32[]{:S(2)}) async-start(bf16[32,24,4096]{2,1,0:T(8,128)(2,1)} %multiply_convert_fusion), calls=%async_computation.2 | async-start | bytes 12582912 | tf_op jit(solution)/shard_map/all_to_all | solution.py:98
  503.0 18.9 %copy-start.1 = (bf16[256,1024]{1,0:T(8,128)(2,1)S(1)}, bf16[256,1024]{1,0:T(8,128)(2,1)}, u32[]{:S(2)}) copy-start(bf16[256,1024]{1,0:T(8,128)(2,1)} %param.13) | copy-start | bytes 1572868
Sparse Core Ops, SparseCore 0:
  10.1 29.1 all-gather.5
  41.2 55.8 all-gather.3
  104.9 75.8 reduce-scatter.1
where the time goes:
time: 536 us; the launch traced here: 528 us
  waiting for transfers between devices  418 us (78%)
  matrix products  42.5 us (8%)
  local copies, waits for them, and re-layouts  25.8 us (5%)
  starting transfers between devices  17.4 us (3%)
  between operations  13.3 us (2%)
  other arithmetic  11 us (2%)
    all_to_all x1, waiting for transfers between devices, body(): lax.all_to_all(computed, ('seq', 'head'), split_axis=0, concat_axis=0, ti...  133 us
    all_to_all x1, waiting for transfers between devices, body(): lax.all_to_all(outgoing, ('seq', 'head'), split_axis=0, concat_axis=0, ti...  132 us
    reduce_scatter x1, waiting for transfers between devices, body(): lax.psum_scatter(jnp.dot(head_normed, full_out, preferred_element_type=jn...  73.3 us
    all_gather x1, waiting for transfers between devices, body(): full_out = lax.all_gather(out_weight, 'seq', axis=1, tiled=True)  50.8 us
    all_gather x1, waiting for transfers between devices, body(): pieces = lax.all_gather(block_state[None], 'seq', axis=0, tiled=True)  28.5 us
    gather x1, local copies, waits for them, and re-layouts, body(): results.reshape(experts * capacity, D)[target].reshape(tok_rows, TOPK, D)  12.3 us
    all_to_all x1, starting transfers between devices, body(): lax.all_to_all(computed, ('seq', 'head'), split_axis=0, concat_axis=0, ti...  11 us
    dot_general x1, matrix products, body(): jnp.einsum('smd,df->smf', slot_rows, gate_weight[0], preferred_element_ty...  10.7 us
  transfers between devices with their start and end apart: 5, of which 5 were waited for; matrix products, arithmetic and copies ran while one was open for 2% of the time, Pallas kernels for 0%

commit v1 on v0

v1 whole, which is shorter than its diff:
```python
import functools

import jax
import jax.numpy as jnp
from jax import lax
from jax.experimental import pallas as pl
from jax.experimental.pallas import tpu as pltpu
from jax.sharding import PartitionSpec as P

HD = 128
TOPK = 8
MESH = pl.DeviceIdType.MESH


def expert_kernel(
    seqs,
    heads,
    chunks,
    scale_ref,
    x_ref,
    res_ref,
    pick_ref,
    mix_ref,
    gate_hbm,
    up_hbm,
    down_hbm,
    out_ref,
    gate_v,
    up_v,
    down_v,
    gath,
    send,
    recv,
    back,
    acc_g,
    acc_u,
    act,
    part,
    psend,
    precv,
    wsem,
    zs,
    zr,
    ps,
    pr,
    rs,
    rr,
    cs,
    cr,
    lsem,
):
    s = lax.axis_index("seq")
    h = lax.axis_index("head")
    rows, width = x_ref.shape
    step = width // chunks
    slots = send.shape[1]
    block = heads * rows

    def cols(c):
        return pl.ds(pl.multiple_of(c * step, step), step)

    def plane(d):
        return lax.rem(s + d, seqs)

    def line(d):
        return lax.rem(h + d, heads)

    def weights(c):
        return (
            pltpu.make_async_copy(gate_hbm.at[0, cols(c), :], gate_v.at[cols(c), :], wsem.at[0, c]),
            pltpu.make_async_copy(up_hbm.at[0, cols(c), :], up_v.at[cols(c), :], wsem.at[1, c]),
            pltpu.make_async_copy(down_hbm.at[0, :, cols(c)], down_v.at[:, cols(c)], wsem.at[2, c]),
        )

    def remote(src, dst, ssem, rsem, seq, head):
        return pltpu.make_async_remote_copy(
            src_ref=src,
            dst_ref=dst,
            send_sem=ssem,
            recv_sem=rsem,
            device_id=(seq, head),
            device_id_type=MESH,
        )

    barrier = pltpu.get_barrier_semaphore()
    for d in range(1, seqs):
        pl.semaphore_signal(barrier, inc=1, device_id=(plane(d), h), device_id_type=MESH)
    for d in range(1, heads):
        pl.semaphore_signal(barrier, inc=1, device_id=(s, line(d)), device_id_type=MESH)

    def start_weights(c, carry):
        gate, up, _ = weights(c)
        gate.start()
        up.start()
        return carry

    def start_down(c, carry):
        weights(c)[2].start()
        return carry

    lax.fori_loop(0, chunks, start_weights, 0)
    lax.fori_loop(0, chunks, start_down, 0)
    gath[h] = x_ref[...]
    pl.semaphore_wait(barrier, seqs + heads - 2)

    def gather_copy(c, d, source, target):
        return remote(
            x_ref.at[:, cols(c)],
            gath.at[source, :, cols(c)],
            zs.at[c, d],
            zr.at[c, source],
            s,
            target,
        )

    def start_gather(c, carry):
        for d in range(1, heads):
            gather_copy(c, d, h, line(d)).start()
        return carry

    lax.fori_loop(0, chunks, start_gather, 0)

    def plane_copy(c, d):
        return remote(
            send.at[plane(d), :, cols(c)], recv.at[s, :, cols(c)], ps.at[c, d], pr.at[c, s],
            plane(d), h,
        )

    def plane_arrival(c, source):
        return remote(
            send.at[source, :, cols(c)], recv.at[source, :, cols(c)], ps.at[c, 0], pr.at[c, source],
            source, h,
        )

    def own_copy(c):
        return pltpu.make_async_copy(
            send.at[s, :, cols(c)], recv.at[s, :, cols(c)], lsem.at[0, c]
        )

    def pick(c):
        for d in range(1, heads):
            gather_copy(c, d, line(d), line(d)).wait_recv()
        picked = jnp.dot(
            pick_ref[...],
            gath[:, :, cols(c)].reshape(block, step),
            preferred_element_type=jnp.float32,
        )
        send[:, :, cols(c)] = picked.astype(jnp.bfloat16).reshape(seqs, slots, step)
        for d in range(1, seqs):
            plane_copy(c, d).start()
        own_copy(c).start()

    acc_g[...] = jnp.zeros_like(acc_g)
    acc_u[...] = jnp.zeros_like(acc_u)

    def expand(c):
        gate, up, _ = weights(c)
        gate.wait()
        up.wait()
        for d in range(1, seqs):
            plane_arrival(c, plane(d)).wait_recv()
        own_copy(c).wait()
        lhs = recv[:, :, cols(c)].reshape(seqs * slots, step)
        acc_g[...] += jnp.dot(lhs, gate_v[cols(c), :], preferred_element_type=jnp.float32)
        acc_u[...] += jnp.dot(lhs, up_v[cols(c), :], preferred_element_type=jnp.float32)

    pick(0)

    def forward(c, carry):
        pick(c)
        expand(c - 1)
        return carry

    lax.fori_loop(1, chunks, forward, 0)
    expand(chunks - 1)

    gate_scale = scale_ref[0, 0]
    up_scale = scale_ref[0, 1]
    down_scale = scale_ref[0, 2]

    def activate(i, carry):
        at = pl.ds(pl.multiple_of(i * slots, slots), slots)
        g = acc_g[at, :] * gate_scale
        act[at, :] = (g / (1.0 + jnp.exp(-g)) * (acc_u[at, :] * up_scale)).astype(jnp.bfloat16)
        return carry

    lax.fori_loop(0, seqs, activate, 0)

    def back_copy(c, d):
        return remote(
            recv.at[plane(d), :, cols(c)], back.at[s, :, cols(c)], rs.at[c, d], rr.at[c, s],
            plane(d), h,
        )

    def back_arrival(c, source):
        return remote(
            recv.at[source, :, cols(c)], back.at[source, :, cols(c)], rs.at[c, 0], rr.at[c, source],
            source, h,
        )

    def own_back(c):
        return pltpu.make_async_copy(
            recv.at[s, :, cols(c)], back.at[s, :, cols(c)], lsem.at[1, c]
        )

    def sum_copy(c, d):
        return remote(
            psend.at[line(d), :, cols(c)], precv.at[h, :, cols(c)], cs.at[c, d], cr.at[c, h],
            s, line(d),
        )

    def sum_arrival(c, source):
        return remote(
            psend.at[source, :, cols(c)], precv.at[source, :, cols(c)], cs.at[c, 0], cr.at[c, source],
            s, source,
        )

    def contract(c):
        weights(c)[2].wait()
        rows_out = jnp.dot(act[...], down_v[:, cols(c)], preferred_element_type=jnp.float32)
        recv[:, :, cols(c)] = (
            (rows_out * down_scale).astype(jnp.bfloat16).reshape(seqs, slots, step)
        )
        for d in range(1, seqs):
            back_copy(c, d).start()
        own_back(c).start()

    def combine(c):
        for d in range(1, seqs):
            back_arrival(c, plane(d)).wait_recv()
        own_back(c).wait()
        total = jnp.dot(
            mix_ref[...],
            back[:, :, cols(c)].reshape(seqs * slots, step),
            preferred_element_type=jnp.float32,
        ).reshape(heads, rows, step)
        part[:, :, cols(c)] = total
        psend[:, :, cols(c)] = total.astype(jnp.bfloat16)
        for d in range(1, heads):
            sum_copy(c, d).start()

    def finish(c):
        total = res_ref[:, cols(c)].astype(jnp.float32) + part[h, :, cols(c)]
        for d in range(1, heads):
            sum_arrival(c, line(d)).wait_recv()
            total = total + precv[line(d), :, cols(c)].astype(jnp.float32)
        out_ref[:, cols(c)] = total.astype(jnp.bfloat16)

    def run_contract(c, carry):
        contract(c)
        return carry

    def run_combine(c, carry):
        combine(c)
        return carry

    def run_finish(c, carry):
        finish(c)
        return carry

    def drain(c, carry):
        for d in range(1, heads):
            gather_copy(c, d, h, line(d)).wait_send()
            sum_copy(c, d).wait_send()
        for d in range(1, seqs):
            plane_copy(c, d).wait_send()
            back_copy(c, d).wait_send()
        return carry

    lax.fori_loop(0, chunks, run_contract, 0)
    lax.fori_loop(0, chunks, run_combine, 0)
    lax.fori_loop(0, chunks, run_finish, 0)
    lax.fori_loop(0, chunks, drain, 0)


def experts_call(seqs, heads, scales, normed, residual, pick, mix, gate, up, down):
    rows, width = normed.shape
    hidden = gate.shape[2]
    slots = pick.shape[0] // seqs
    chunks = 4
    vmem = pl.BlockSpec(memory_space=pltpu.VMEM)
    anywhere = pl.BlockSpec(memory_space=pl.ANY)
    bf, f32 = jnp.bfloat16, jnp.float32
    dma = pltpu.SemaphoreType.DMA
    return pl.pallas_call(
        functools.partial(expert_kernel, seqs, heads, chunks),
        out_shape=jax.ShapeDtypeStruct((rows, width), bf),
        in_specs=[pl.BlockSpec(memory_space=pltpu.SMEM)] + [vmem] * 4 + [anywhere] * 3,
        out_specs=vmem,
        scratch_shapes=[
            pltpu.VMEM((width, hidden), bf),
            pltpu.VMEM((width, hidden), bf),
            pltpu.VMEM((hidden, width), bf),
            pltpu.VMEM((heads, rows, width), bf),
            pltpu.VMEM((seqs, slots, width), bf),
            pltpu.VMEM((seqs, slots, width), bf),
            pltpu.VMEM((seqs, slots, width), bf),
            pltpu.VMEM((seqs * slots, hidden), f32),
            pltpu.VMEM((seqs * slots, hidden), f32),
            pltpu.VMEM((seqs * slots, hidden), bf),
            pltpu.VMEM((heads, rows, width), f32),
            pltpu.VMEM((heads, rows, width), bf),
            pltpu.VMEM((heads, rows, width), bf),
            dma((3, chunks)),
            dma((chunks, heads)),
            dma((chunks, heads)),
            dma((chunks, seqs)),
            dma((chunks, seqs)),
            dma((chunks, seqs)),
            dma((chunks, seqs)),
            dma((chunks, heads)),
            dma((chunks, heads)),
            dma((2, chunks)),
        ],
        compiler_params=pltpu.CompilerParams(
            collective_id=0, has_side_effects=True, vmem_limit_bytes=60 * 1024 * 1024
        ),
    )(scales, normed, residual, pick, mix, gate, up, down)


def routing(expert_ids, expert_gates, seqs, heads):
    tok_rows = expert_ids.shape[0]
    capacity = 3 * tok_rows * TOPK // (2 * seqs * heads)
    slots = -(-capacity * heads // 16) * 16
    routed = jnp.concatenate([expert_ids.astype(jnp.float32), expert_gates], axis=1)
    routed = lax.all_gather(routed, "head", axis=0, tiled=True).T
    ids, gates = routed[:TOPK], routed[TOPK:]
    tokens = routed.shape[1]
    mine = (jnp.arange(seqs) * heads + lax.axis_index("head")).astype(jnp.float32)
    chosen = ids[None] == mine[:, None, None]
    hit = jnp.any(chosen, axis=1)
    weight = jnp.sum(jnp.where(chosen, gates[None], 0.0), axis=1)
    earlier = jnp.triu(jnp.ones((tokens, tokens), jnp.bfloat16), 1)
    rank = jnp.dot(hit.astype(jnp.bfloat16), earlier, preferred_element_type=jnp.float32)
    place = jnp.where(hit, rank, -1.0)
    slot = jnp.arange(slots, dtype=jnp.float32)
    taken = place[:, None, :] == slot[None, :, None]
    pick = taken.astype(jnp.bfloat16).reshape(seqs * slots, tokens)
    taken_t = place.T[:, :, None] == slot[None, None, :]
    mix = jnp.where(taken_t, weight.T[:, :, None], 0.0).astype(jnp.bfloat16)
    return pick, mix.reshape(tokens, seqs * slots)


def body(
    query,
    key,
    value,
    head_gain,
    out_weight,
    stream,
    model_gain,
    expert_ids,
    expert_gates,
    gate_weight,
    up_weight,
    down_weight,
    weight_scales,
):
    seqs, heads = lax.axis_size("seq"), lax.axis_size("head")
    pick, mix = routing(expert_ids, expert_gates, seqs, heads)
    seq_rows = query.shape[0]
    heads_local = head_gain.shape[0] // HD
    query_rows = query.reshape(seq_rows, heads_local, HD)
    key_rows = key.reshape(seq_rows, heads_local, HD)
    value_rows = value.reshape(seq_rows, heads_local, HD)
    scores = jnp.einsum("thd,shd->hts", query_rows, key_rows, preferred_element_type=jnp.float32)
    causal = jnp.tril(jnp.ones((seq_rows, seq_rows), dtype=bool))
    scores = jnp.where(causal[None, :, :], scores, 0.0).astype(jnp.bfloat16)
    local_part = jnp.einsum("hts,shd->thd", scores, value_rows, preferred_element_type=jnp.float32)
    block_state = jnp.einsum(
        "shd,she->hde", key_rows, value_rows, preferred_element_type=jnp.float32
    )
    position = lax.axis_index("seq")
    pieces = lax.all_gather(block_state[None], "seq", axis=0, tiled=True)
    piece_count = pieces.shape[0]
    selected = (jnp.arange(piece_count, dtype=jnp.int32) < position).astype(jnp.float32)
    prior_state = jnp.einsum("n,nhde->hde", selected, pieces)
    earlier_part = jnp.einsum(
        "thd,hde->the",
        query_rows,
        prior_state.astype(jnp.bfloat16),
        preferred_element_type=jnp.float32,
    )
    mixed_heads = local_part + earlier_part
    mean_square = jnp.mean(mixed_heads * mixed_heads, axis=-1, keepdims=True)
    head_normed = (
        mixed_heads * lax.rsqrt(mean_square + 1e-06) * head_gain.reshape(heads_local, HD)
    ).astype(jnp.bfloat16)
    head_normed = head_normed.reshape(seq_rows, heads_local * HD)
    full_out = lax.all_gather(out_weight, "seq", axis=1, tiled=True)
    attention = lax.psum_scatter(
        jnp.dot(head_normed, full_out, preferred_element_type=jnp.float32),
        "head",
        scatter_dimension=0,
        tiled=True,
    )
    residual = (stream.astype(jnp.float32) + attention).astype(jnp.bfloat16)
    residual_float = residual.astype(jnp.float32)
    mean_square = jnp.mean(residual_float * residual_float, axis=-1, keepdims=True)
    normed = (residual_float * lax.rsqrt(mean_square + 1e-06) * model_gain).astype(jnp.bfloat16)
    return experts_call(
        seqs,
        heads,
        weight_scales,
        normed,
        residual,
        pick,
        mix,
        gate_weight,
        up_weight,
        down_weight,
    )


def solution(mesh):
    return jax.shard_map(
        body,
        mesh=mesh,
        in_specs=(
            P("seq", "head"),
            P("seq", "head"),
            P("seq", "head"),
            P("head"),
            P("head", "seq"),
            P(("seq", "head"), None),
            P(),
            P(("seq", "head"), None),
            P(("seq", "head"), None),
            P(("seq", "head"), None, None),
            P(("seq", "head"), None, None),
            P(("seq", "head"), None, None),
            P(("seq", "head"), None),
        ),
        out_specs=P(("seq", "head"), None),
        check_vma=False,
    )
```

time: 536 us -> 369 us (0.69); the launches traced: 528 us -> 368 us
  waiting for transfers between devices: 418 us -> 142 us
  Pallas kernels: 0 us -> 176 us
  matrix products: 42.5 us -> 15 us
  local copies, waits for them, and re-layouts: 25.8 us -> 4.96 us
  starting transfers between devices: 17.4 us -> 0.08 us
  blocking collectives: 0 us -> 12.3 us
  other arithmetic: 11 us -> 4.69 us
    all_to_all x2 -> x0, waiting for transfers between devices: 265 us -> none  [the longest x1 133 us: body(): lax.all_to_all(computed, ('seq', 'head'), split_axis=0, concat_axis=0, ti...]
    pallas_call x0 -> x1, Pallas kernels: none -> 176 us  [experts_call(): pl.pallas_call(functools.partial(expert_kernel, seqs, heads, chunks), out...]
    dot_general x3 -> x1, matrix products: 27.6 us -> 0.14 us  [routing(): jnp.dot(hit.astype(jnp.bfloat16), earlier, preferred_element_type=jnp.flo...]
    all_to_all x2 -> x0, starting transfers between devices: 17.3 us -> none  [the longest x1 11 us: body(): lax.all_to_all(computed, ('seq', 'head'), split_axis=0, concat_axis=0, ti...]
    reduce_scatter x1, waiting for transfers between devices: 73.3 us -> 60.5 us  [body(): lax.psum_scatter(jnp.dot(head_normed, full_out, preferred_element_type=jn...]
    all_gather x0 -> x1, blocking collectives: none -> 12.3 us  [routing(): routed = lax.all_gather(routed, 'head', axis=0, tiled=True).T]
    gather x1 -> x0, local copies, waits for them, and re-layouts: 12.3 us -> none  [body(): results.reshape(experts * capacity, D)[target].reshape(tok_rows, TOPK, D)]
    scatter x1 -> x0, local copies, waits for them, and re-layouts: 9.77 us -> none  [body(): jnp.zeros((experts * capacity, D), jnp.bfloat16).at[target].set(source_rows)]
  transfers between devices with their start and end apart: 5 -> 3, of which waited for: 5 -> 3; matrix products, arithmetic and copies ran while one was open for 2% -> 2% of each run, Pallas kernels for 0% -> 0%
where the time goes in v1:
time: 369 us; the launch traced here: 368 us
  Pallas kernels  176 us (48%)
  waiting for transfers between devices  142 us (38%)
  matrix products  15 us (4%)
  between operations  13.3 us (4%)
  blocking collectives  12.3 us (3%)
  local copies, waits for them, and re-layouts  4.96 us (1%)
  other arithmetic  4.69 us (1%)
    pallas_call x1, Pallas kernels, experts_call(): pl.pallas_call(functools.partial(expert_kernel, seqs, heads, chunks), out...  176 us
    reduce_scatter x1, waiting for transfers between devices, body(): lax.psum_scatter(jnp.dot(head_normed, full_out, preferred_element_type=jn...  60.5 us
    all_gather x1, waiting for transfers between devices, body(): full_out = lax.all_gather(out_weight, 'seq', axis=1, tiled=True)  52.1 us
    all_gather x1, waiting for transfers between devices, body(): pieces = lax.all_gather(block_state[None], 'seq', axis=0, tiled=True)  28.5 us
    all_gather x1, blocking collectives, routing(): routed = lax.all_gather(routed, 'head', axis=0, tiled=True).T  12.3 us
    dot_general x1, matrix products, body(): jnp.dot(head_normed, full_out, preferred_element_type=jnp.float32)  7.7 us
  transfers between devices with their start and end apart: 3, of which 3 were waited for; matrix products, arithmetic and copies ran while one was open for 2% of the time, Pallas kernels for 0%

profile of v1, /device:TPU:25, one launch (start us, length us, event | category | flops | bytes accessed | tf_op | source)
XLA Modules:
  0.0 368.1 jit_solution(13989696854404709001)
XLA Ops:
  6.5 1.3 copy.49
  7.8 2.0 fusion.12
  10.0 0.7 all-gather.5.cloned.1.call-update
  10.7 28.5 %all-gather.7.cloned.1.call-done = bf16[64,128,128]{2,1,0:T(8,128)(2,1)} async-done(((bf16[8,128,128]{2,1,0:T(8,128)(2,1)}), bf16[64,128,128]{2,1,0:T(8,128)(2,1)}) %all-gather.7.cloned.1.call-update) | async-done | bytes 2097168 | tf_op jit(solution)/shard_map/all_gather | solution.py:374
  39.2 3.0 fusion
  42.2 0.4 copy.48
  42.6 0.3 convolution_bitcast_fusion
  42.9 1.8 multiply_reduce_fusion
  44.7 0.2 multiply_convert_fusion
  44.9 52.1 %all-gather.5.cloned.1.call-done = bf16[1024,4096]{1,0:T(8,128)(2,1)} async-done(((bf16[1024,512]{1,0:T(8,128)(2,1)}), bf16[1024,4096]{1,0:T(8,128)(2,1)}) %all-gather.5.cloned.1.call-update) | async-done | bytes 8388624 | tf_op jit(solution)/shard_map/all_gather | solution.py:390
  97.0 7.7 %fusion.36 = f32[256,4096]{1,0:T(8,128)} fusion(bf16[256,1024]{0,1:T(8,128)(2,1)S(1)} %bitcast.67, bf16[1024,4096]{1,0:T(8,128)(2,1)} %all-gather.5.cloned.1.call-done), kind=kOutput, calls=%fused_computation.50 | convolution fusion | flops 2147483648 | bytes 13107200 | tf_op jit(solution)/shard_map/dot_general | solution.py:392
  104.7 0.7 copy-done.5
  105.4 12.3 %all-gather.1 = f32[4,64,16]{1,2,0:T(8,128)S(1)} all-gather(f32[1,64,16]{1,2,0:T(8,128)S(1)} %maximum_bitcast_fusion), channel_id=1, replica_groups=mesh['seq'=8,'head'=4] {'head'}, dimensions={0}, use_global_device_ids=true | all-gather | bytes 20480 | tf_op jit(solution)/shard_map/all_gather | solution.py:326
  117.9 0.1 compare_reduce_fusion
  118.0 0.1 convolution_select_fusion
  118.2 0.3 copy.44
  118.6 0.2 copy.45
  118.9 0.9 fusion.10.pick_ref
  119.8 0.8 select_convert_fusion.1.mix_ref
  120.6 60.5 %reduce-scatter.2.cloned.1.call-done = f32[64,4096]{1,0:T(8,128)} async-done(((f32[256,4096]{1,0:T(8,128)}), f32[64,4096]{1,0:T(8,128)}) %reduce-scatter.2.cloned.1.call-update) | async-done | bytes 1048592 | tf_op jit(solution)/shard_map/reduce_scatter | solution.py:391
  181.1 1.5 fusion.5
  182.6 1.0 fusion.7.x_ref
  183.6 176.1 %shard_map.127 = bf16[64,4096]{1,0:T(8,128)(2,1)} custom-call(f32[1,3]{1,0:T(1,128)} %scale_ref.1, bf16[64,4096]{1,0:T(8,128)(2,1)} %fusion.7.x_ref, bf16[64,4096]{1,0:T(8,128)(2,1)} %copy-done.1, bf16[768,256]{1,0:T(8,128)(2,1)} %fusion.10.pick_ref, bf16[256,768]{1,0:T(8,128)(2,1)} %select_convert_fusion.1.mix_ref, bf16[1,4096,768]{2,1,0:T(8,128)(2,1)} %gate_hbm.1, ...), custom_call_target="tpu_custom_call" | custom-call | tf_op jit(solution)/shard_map/pallas_call | solution.py:285
  359.7 1.9 copy.76
  (32 shorter events, 0.6 us)
Async XLA Ops:
  6.5 36.1 %copy-start = (bf16[256,1024]{1,0:T(8,128)(2,1)S(1)}, bf16[256,1024]{1,0:T(8,128)(2,1)}, u32[]{:S(2)}) copy-start(bf16[256,1024]{1,0:T(8,128)(2,1)} %param.13) | copy-start | bytes 1572868
  6.5 32.7 %all-gather.7.cloned.1.call-start = ((), (), s32[]{:S(2)}) async-start(), calls=%async_computation.3 | async-start | bytes 2359296 | tf_op jit(solution)/shard_map/all_gather | solution.py:374
  9.9 87.1 %all-gather.5.cloned.1.call-start = ((), (), s32[]{:S(2)}) async-start(), calls=%async_computation.1 | async-start | bytes 9437184 | tf_op jit(solution)/shard_map/all_gather | solution.py:390
  10.7 170.5 %reduce-scatter.2.cloned.1.call-start = ((), (), s32[]{:S(2)}) async-start(), calls=%async_computation.2 | async-start | bytes 5242880 | tf_op jit(solution)/shard_map/reduce_scatter | solution.py:391
  39.2 5.5 %copy-start.4 = (f32[1024]{0:T(1024)S(1)}, f32[1024]{0:T(1024)}, u32[]{:S(2)}) copy-start(f32[1024]{0:T(1024)} %param.16) | copy-start | bytes 12292
  104.7 0.7 copy-start.5
  104.7 0.7 copy-start.6
  104.7 76.4 %copy-start.2 = (bf16[64,4096]{1,0:T(8,128)(2,1)S(1)}, bf16[64,4096]{1,0:T(8,128)(2,1)}, u32[]{:S(2)}) copy-start(bf16[64,4096]{1,0:T(8,128)(2,1)} %param.18) | copy-start | bytes 1572868
  105.4 77.2 %copy-start.3 = (f32[4096]{0:T(1024)S(1)}, f32[4096]{0:T(1024)}, u32[]{:S(2)}) copy-start(f32[4096]{0:T(1024)} %param.19) | copy-start | bytes 49156
  182.6 1.0 copy-start.1
Sparse Core Ops, SparseCore 0:
  10.0 29.1 all-gather.6
  41.1 55.8 all-gather.4
  104.9 76.2 reduce-scatter.1

commit v2 on v1

--- a/solution.py
+++ b/solution.py
@@ -318,12 +318,318 @@
     )(scales, normed, residual, pick, mix, gate, up, down)
 
 
-def routing(expert_ids, expert_gates, seqs, heads):
-    tok_rows = expert_ids.shape[0]
+def attention_kernel(
+    seqs,
+    heads,
+    halves,
+    q_ref,
+    k_ref,
+    v_ref,
+    gain_ref,
+    w_hbm,
+    stream_ref,
+    model_ref,
+    route_ref,
+    res_ref,
+    normed_ref,
+    routes_ref,
+    state,
+    mixed,
+    normed_heads,
+    wbuf,
+    own,
+    psend,
+    precv,
+    routes,
+    sds,
+    sdr,
+    sfs,
+    sfr,
+    wds,
+    wdr,
+    wfs,
+    wfr,
+    zs,
+    zr,
+    gs,
+    gr,
+    lsem,
+):
+    s = lax.axis_index("seq")
+    h = lax.axis_index("head")
+    tokens = q_ref.shape[0]
+    rows, width = stream_ref.shape
+    local = q_ref.shape[1] // HD
+    block = w_hbm.shape[1]
+    part = block // halves
+
+    def flip(d):
+        out, bit = s, 1
+        while bit < seqs:
+            if d & bit:
+                out = out + bit * (1 - 2 * ((s // bit) % 2))
+            bit *= 2
+        return out
+
+    partner = flip(1)
+
+    def line(d):
+        return lax.rem(h + d, heads)
+
+    def remote(src, dst, ssem, rsem, seq, head):
+        return pltpu.make_async_remote_copy(
+            src_ref=src,
+            dst_ref=dst,
+            send_sem=ssem,
+            recv_sem=rsem,
+            device_id=(seq, head),
+            device_id_type=MESH,
+        )
+
+    def state_direct(slot, peer):
+        return remote(state.at[slot], state.at[slot], sds.at[peer], sdr.at[slot], peer, h)
+
+    def state_pass(slot):
+        return remote(state.at[slot], state.at[slot], sfs.at[slot], sfr.at[slot], partner, h)
+
+    def w_at(slot, half):
+        return wbuf.at[slot, :, pl.ds(half * part, part)]
+
+    def w_direct(slot, half, peer):
+        return remote(
+            w_hbm.at[:, pl.ds(half * part, part)], w_at(slot, half),
+            wds.at[peer, half], wdr.at[slot, half], peer, h,
+        )
+
+    def w_pass(slot, half):
+        return remote(
+            w_at(slot, half), w_at(slot, half), wfs.at[slot, half], wfr.at[slot, half], partner, h
+        )
+
+    def w_own_pass(half):
+        return remote(
+            w_hbm.at[:, pl.ds(half * part, part)], w_at(s, half),
+            wfs.at[s, half], wfr.at[s, half], partner, h,
+        )
+
+    def w_own():
+        return pltpu.make_async_copy(w_hbm, wbuf.at[s], lsem.at[0])
+
+    def route_copy(slot, target):
+        return remote(route_ref, routes.at[slot], gs.at[target], gr.at[slot], s, target)
+
+    barrier = pltpu.get_barrier_semaphore()
+    for d in range(1, seqs):
+        pl.semaphore_signal(barrier, inc=1, device_id=(flip(d), h), device_id_type=MESH)
+    for d in range(1, heads):
+        pl.semaphore_signal(barrier, inc=1, device_id=(s, line(d)), device_id_type=MESH)
+    w_own().start()
+    routes[h] = route_ref[...]
+
+    def lanes(i):
+        return pl.ds(pl.multiple_of(i * HD, HD), HD)
+
+    def block_state(i, carry):
+        total = lax.dot_general(
+            k_ref[:, lanes(i)], v_ref[:, lanes(i)], (((0,), (0,)), ((), ())),
+            preferred_element_type=jnp.float32,
+        )
+        state[s, i] = total.astype(jnp.bfloat16)
+        return carry
+
+    lax.fori_loop(0, local, block_state, 0)
+    pl.semaphore_wait(barrier, seqs + heads - 2)
+    for d in range(2, seqs, 2):
+        state_direct(s, flip(d)).start()
+    state_pass(s).start()
+    for d in range(1, heads):
+        route_copy(h, line(d)).start()
+    for half in range(halves):
+        w_own_pass(half).start()
+        for d in range(2, seqs, 2):
+            w_direct(s, half, flip(d)).start()
+
+    row = lax.broadcasted_iota(jnp.int32, (tokens, tokens), 0)
+    col = lax.broadcasted_iota(jnp.int32, (tokens, tokens), 1)
+    causal = col <= row
+
+    def local_part(i, carry):
+        scores = lax.dot_general(
+            q_ref[:, lanes(i)], k_ref[:, lanes(i)], (((1,), (1,)), ((), ())),
+            preferred_element_type=jnp.float32,
+        )
+        scores = jnp.where(causal, scores, 0.0).astype(jnp.bfloat16)
+        mixed[:, lanes(i)] = jnp.dot(
+            scores, v_ref[:, lanes(i)], preferred_element_type=jnp.float32
+        )
+        return carry
+
+    lax.fori_loop(0, local, local_part, 0)
+
+    for d in range(2, seqs, 2):
+        state_direct(flip(d), flip(d)).wait_recv()
+        state_pass(flip(d)).start()
+    for d in range(1, seqs, 2):
+        state_pass(flip(d)).wait_recv()
+
+    def earlier_part(i, carry):
+        prior = jnp.zeros((HD, HD), jnp.float32)
+        for c in range(seqs):
+            prior = prior + jnp.where(c < s, state[c, i].astype(jnp.float32), 0.0)
+        total = mixed[:, lanes(i)] + jnp.dot(
+            q_ref[:, lanes(i)], prior.astype(jnp.bfloat16), preferred_element_type=jnp.float32
+        )
+        mean_square = jnp.mean(total * total, axis=-1, keepdims=True)
+        normed_heads[:, lanes(i)] = (
+            total * lax.rsqrt(mean_square + 1e-06) * gain_ref[:, lanes(i)]
+        ).astype(jnp.bfloat16)
+        return carry
+
+    lax.fori_loop(0, local, earlier_part, 0)
+
+    def cols(slot, half):
+        return pl.ds(pl.multiple_of(slot * block + half * part, part), part)
+
+    def sum_copy(slot, half, d):
+        return remote(
+            psend.at[line(d), :, cols(slot, half)], precv.at[h, :, cols(slot, half)],
+            zs.at[slot, half, d], zr.at[slot, half, h], s, line(d),
+        )
+
+    def sum_arrival(slot, half, source):
+        return remote(
+            psend.at[source, :, cols(slot, half)], precv.at[source, :, cols(slot, half)],
+            zs.at[slot, half, 0], zr.at[slot, half, source], s, source,
+        )
+
+    def project(slot, half):
+        total = jnp.dot(
+            normed_heads[...],
+            wbuf[slot, :, pl.ds(half * part, part)],
+            preferred_element_type=jnp.float32,
+        ).reshape(heads, rows, part)
+        own[:, :, cols(slot, half)] = total
+        psend[:, :, cols(slot, half)] = total.astype(jnp.bfloat16)
+        for d in range(1, heads):
+            sum_copy(slot, half, d).start()
+
+    w_own().wait()
+    for half in range(halves):
+        for d in range(0, seqs, 2):
+            if d:
+                w_direct(flip(d), half, flip(d)).wait_recv()
+                w_pass(flip(d), half).start()
+            project(flip(d), half)
+            w_pass(flip(d + 1), half).wait_recv()
+            project(flip(d + 1), half)
+
+    def settle(i, carry):
+        for half in range(halves):
+            for d in range(1, heads):
+                sum_arrival(i, half, line(d)).wait_recv()
+        return carry
+
+    lax.fori_loop(0, seqs, settle, 0)
+    for d in range(1, heads):
+        route_copy(line(d), line(d)).wait_recv()
+    routes_ref[...] = routes[...]
+
+    group = 16
+
+    def normalise(i, carry):
+        at = pl.ds(pl.multiple_of(i * group, group), group)
+        total = own[h, at, :]
+        for d in range(1, heads):
+            total = total + precv[line(d), at, :].astype(jnp.float32)
+        residual = (stream_ref[at, :].astype(jnp.float32) + total).astype(jnp.bfloat16)
+        res_ref[at, :] = residual
+        value = residual.astype(jnp.float32)
+        mean_square = jnp.mean(value * value, axis=-1, keepdims=True)
+        normed_ref[at, :] = (
+            value * lax.rsqrt(mean_square + 1e-06) * model_ref[...]
+        ).astype(jnp.bfloat16)
+        return carry
+
+    lax.fori_loop(0, rows // group, normalise, 0)
+
+    for d in range(2, seqs, 2):
+        state_direct(s, flip(d)).wait_send()
+        for half in range(halves):
+            w_direct(s, half, flip(d)).wait_send()
+    for d in range(0, seqs, 2):
+        state_pass(flip(d)).wait_send()
+        for half in range(halves):
+            if d:
+                w_pass(flip(d), half).wait_send()
+            else:
+                w_own_pass(half).wait_send()
+    for d in range(1, heads):
+        route_copy(h, line(d)).wait_send()
+
+    def drain(i, carry):
+        for half in range(halves):
+            for d in range(1, heads):
+                sum_copy(i, half, d).wait_send()
+        return carry
+
+    lax.fori_loop(0, seqs, drain, 0)
+
+
+def attention_call(seqs, heads, query, key, value, gain, weight, stream, model_gain, route):
+    tokens, features = query.shape
+    rows, width = stream.shape
+    local = features // HD
+    block = weight.shape[1]
+    halves = 2
+    vmem = pl.BlockSpec(memory_space=pltpu.VMEM)
+    anywhere = pl.BlockSpec(memory_space=pl.ANY)
+    bf, f32 = jnp.bfloat16, jnp.float32
+    dma = pltpu.SemaphoreType.DMA
+    return pl.pallas_call(
+        functools.partial(attention_kernel, seqs, heads, halves),
+        out_shape=(
+            jax.ShapeDtypeStruct((rows, width), bf),
+            jax.ShapeDtypeStruct((rows, width), bf),
+            jax.ShapeDtypeStruct((heads,) + route.shape, f32),
+        ),
+        in_specs=[vmem] * 4 + [anywhere] + [vmem] * 3,
+        out_specs=(vmem,) * 3,
+        scratch_shapes=[
+            pltpu.VMEM((seqs, local, HD, HD), bf),
+            pltpu.VMEM((tokens, features), f32),
+            pltpu.VMEM((tokens, features), bf),
+            pltpu.VMEM((seqs, features, block), bf),
+            pltpu.VMEM((heads, rows, width), f32),
+            pltpu.VMEM((heads, rows, width), bf),
+            pltpu.VMEM((heads, rows, width), bf),
+            pltpu.VMEM((heads,) + route.shape, f32),
+            dma((seqs,)),
+            dma((seqs,)),
+            dma((seqs,)),
+            dma((seqs,)),
+            dma((seqs, halves)),
+            dma((seqs, halves)),
+            dma((seqs, halves)),
+            dma((seqs, halves)),
+            dma((seqs, halves, heads)),
+            dma((seqs, halves, heads)),
+            dma((heads,)),
+            dma((heads,)),
+            dma((1,)),
+        ],
+        compiler_params=pltpu.CompilerParams(
+            collective_id=1, has_side_effects=True, vmem_limit_bytes=50000 * 1024
+        ),
+    )(
+        query, key, value, gain.reshape(1, -1), weight, stream, model_gain.reshape(1, -1), route
+    )
+
+
+def routing(routed, seqs, heads):
+    tok_rows = routed.shape[1]
     capacity = 3 * tok_rows * TOPK // (2 * seqs * heads)
     slots = -(-capacity * heads // 16) * 16
-    routed = jnp.concatenate([expert_ids.astype(jnp.float32), expert_gates], axis=1)
-    routed = lax.all_gather(routed, "head", axis=0, tiled=True).T
+    routed = routed.reshape(-1, 2 * TOPK).T
     ids, gates = routed[:TOPK], routed[TOPK:]
     tokens = routed.shape[1]
     mine = (jnp.arange(seqs) * heads + lax.axis_index("head")).astype(jnp.float32)
@@ -357,47 +663,11 @@
     weight_scales,
 ):
     seqs, heads = lax.axis_size("seq"), lax.axis_size("head")
-    pick, mix = routing(expert_ids, expert_gates, seqs, heads)
-    seq_rows = query.shape[0]
-    heads_local = head_gain.shape[0] // HD
-    query_rows = query.reshape(seq_rows, heads_local, HD)
-    key_rows = key.reshape(seq_rows, heads_local, HD)
-    value_rows = value.reshape(seq_rows, heads_local, HD)
-    scores = jnp.einsum("thd,shd->hts", query_rows, key_rows, preferred_element_type=jnp.float32)
-    causal = jnp.tril(jnp.ones((seq_rows, seq_rows), dtype=bool))
-    scores = jnp.where(causal[None, :, :], scores, 0.0).astype(jnp.bfloat16)
-    local_part = jnp.einsum("hts,shd->thd", scores, value_rows, preferred_element_type=jnp.float32)
-    block_state = jnp.einsum(
-        "shd,she->hde", key_rows, value_rows, preferred_element_type=jnp.float32
+    route = jnp.concatenate([expert_ids.astype(jnp.float32), expert_gates], axis=1)
+    residual, normed, routed = attention_call(
+        seqs, heads, query, key, value, head_gain, out_weight, stream, model_gain, route
     )
-    position = lax.axis_index("seq")
-    pieces = lax.all_gather(block_state[None], "seq", axis=0, tiled=True)
-    piece_count = pieces.shape[0]
-    selected = (jnp.arange(piece_count, dtype=jnp.int32) < position).astype(jnp.float32)
-    prior_state = jnp.einsum("n,nhde->hde", selected, pieces)
-    earlier_part = jnp.einsum(
-        "thd,hde->the",
-        query_rows,
-        prior_state.astype(jnp.bfloat16),
-        preferred_element_type=jnp.float32,
-    )
-    mixed_heads = local_part + earlier_part
-    mean_square = jnp.mean(mixed_heads * mixed_heads, axis=-1, keepdims=True)
-    head_normed = (
-        mixed_heads * lax.rsqrt(mean_square + 1e-06) * head_gain.reshape(heads_local, HD)
-    ).astype(jnp.bfloat16)
-    head_normed = head_normed.reshape(seq_rows, heads_local * HD)
-    full_out = lax.all_gather(out_weight, "seq", axis=1, tiled=True)
-    attention = lax.psum_scatter(
-        jnp.dot(head_normed, full_out, preferred_element_type=jnp.float32),
-        "head",
-        scatter_dimension=0,
-        tiled=True,
-    )
-    residual = (stream.astype(jnp.float32) + attention).astype(jnp.bfloat16)
-    residual_float = residual.astype(jnp.float32)
-    mean_square = jnp.mean(residual_float * residual_float, axis=-1, keepdims=True)
-    normed = (residual_float * lax.rsqrt(mean_square + 1e-06) * model_gain).astype(jnp.bfloat16)
+    pick, mix = routing(routed, seqs, heads)
     return experts_call(
         seqs,
         heads,

time: 369 us -> 266 us (0.72)
  waiting for transfers between devices: 142 us -> 0 us
  Pallas kernels: 176 us -> 251 us
  matrix products: 15 us -> 0.14 us
  between operations: 13.3 us -> 0.09 us
  blocking collectives: 12.3 us -> 0 us
  local copies, waits for them, and re-layouts: 4.96 us -> 11.2 us
    all_gather x2 -> x0, waiting for transfers between devices: 80.5 us -> none  [the longest x1 52.1 us: body(): full_out = lax.all_gather(out_weight, 'seq', axis=1, tiled=True)]
    pallas_call x0 -> x1, Pallas kernels: none -> 76 us  [attention_call(): pl.pallas_call(functools.partial(attention_kernel, seqs, heads, halves),...]
    reduce_scatter x1 -> x0, waiting for transfers between devices: 60.5 us -> none  [body(): lax.psum_scatter(jnp.dot(head_normed, full_out, preferred_element_type=jn...]
    dot_general x5 -> x0, matrix products: 14.8 us -> none  [the longest x1 7.7 us: body(): jnp.dot(head_normed, full_out, preferred_element_type=jnp.float32)]
    all_gather x1 -> x0, blocking collectives: 12.3 us -> none  [routing(): routed = lax.all_gather(routed, 'head', axis=0, tiled=True).T]
    unnamed x16 -> x19, local copies, waits for them, and re-layouts: 2.65 us -> 10.2 us
  transfers between devices with their start and end apart: 3 -> 0, of which waited for: 3 -> 0; matrix products, arithmetic and copies ran while one was open for 2% -> 0% of each run, Pallas kernels for 0% -> 0%
where the time goes in v2:
time: 266 us; the launch traced here: 265 us
  Pallas kernels  251 us (94%)
  local copies, waits for them, and re-layouts  11.2 us (4%)
  other arithmetic  3.36 us (1%)
    pallas_call x1, Pallas kernels, experts_call(): pl.pallas_call(functools.partial(expert_kernel, seqs, heads, chunks), out...  175 us
    pallas_call x1, Pallas kernels, attention_call(): pl.pallas_call(functools.partial(attention_kernel, seqs, heads, halves),...  76 us
    unnamed x19, local copies, waits for them, and re-layouts  10.2 us

profile of v2, /device:TPU:25, one launch (start us, length us, event | category | flops | bytes accessed | tf_op | source)
XLA Modules:
  0.0 265.4 jit_solution(8675198039243716553)
XLA Ops:
  0.0 0.7 convert_element_type.19
  0.7 0.7 pad_maximum_fusion
  1.4 0.1 copy.30.route_ref
  1.5 1.2 copy-done
  2.7 1.0 copy-done.1
  3.7 1.0 copy-done.2
  4.8 1.0 copy-done.3
  5.8 1.0 copy-done.4
  6.9 0.7 copy-done.7
  7.6 0.7 copy-done.8
  8.3 76.0 %shard_map.127 = (bf16[64,4096]{1,0:T(8,128)(2,1)S(1)}, bf16[64,4096]{1,0:T(8,128)(2,1)S(1)}, f32[4,64,16]{2,1,0:T(8,128)S(1)}) custom-call(bf16[256,1024]{1,0:T(8,128)(2,1)S(1)} %copy-done.1, bf16[256,1024]{1,0:T(8,128)(2,1)S(1)} %copy-done.2, bf16[256,1024]{1,0:T(8,128)(2,1)S(1)} %copy-done.3, f32[1,1024]{1,0:T(1,128)S(1)} %bitcast.16, ...), custom_call_target="tpu_custom_call" | custom-call | tf_op jit(solution)/shard_map/pallas_call | solution.py:588
  84.3 0.8 copy-done.5
  85.0 0.8 copy-done.6
  85.8 0.1 fusion.8
  86.1 0.1 fusion.3
  86.2 0.2 copy.34
  86.4 0.1 compare_reduce_fusion
  86.5 0.1 convolution_select_fusion
  86.7 0.3 copy.32
  87.0 0.1 eq.59
  87.1 0.8 select_convert_fusion.mix_ref
  87.9 0.9 fusion.pick_ref
  88.9 174.7 %shard_map.128 = bf16[64,4096]{1,0:T(8,128)(2,1)} custom-call(f32[1,3]{1,0:T(1,128)} %scale_ref.1, bf16[64,4096]{1,0:T(8,128)(2,1)} %copy-done.6, bf16[64,4096]{1,0:T(8,128)(2,1)} %copy-done.5, bf16[768,256]{1,0:T(8,128)(2,1)} %fusion.pick_ref, bf16[256,768]{1,0:T(8,128)(2,1)} %select_convert_fusion.mix_ref, bf16[1,4096,768]{2,1,0:T(8,128)(2,1)} %gate_hbm.1, ...), custom_call_target="tpu_custom_call" | custom-call | tf_op jit(solution)/shard_map/pallas_call | solution.py:285
  263.6 1.9 copy.36
  (15 shorter events, 0.3 us)
Async XLA Ops:
  1.5 1.2 copy-start
  2.7 1.0 copy-start.1
  3.7 1.0 copy-start.2
  4.8 1.0 copy-start.3
  5.8 1.0 copy-start.4
  6.9 0.7 copy-start.7
  7.6 0.7 copy-start.8
  84.3 0.8 copy-start.5
  85.0 0.8 copy-start.6

commit v3 on v2

--- a/solution.py
+++ b/solution.py
@@ -277,7 +277,7 @@
     rows, width = normed.shape
     hidden = gate.shape[2]
     slots = pick.shape[0] // seqs
-    chunks = 4
+    chunks = 8
     vmem = pl.BlockSpec(memory_space=pltpu.VMEM)
     anywhere = pl.BlockSpec(memory_space=pl.ANY)
     bf, f32 = jnp.bfloat16, jnp.float32
@@ -322,17 +322,21 @@
     seqs,
     heads,
     halves,
-    q_ref,
-    k_ref,
-    v_ref,
+    q_hbm,
+    k_hbm,
+    v_hbm,
     gain_ref,
     w_hbm,
-    stream_ref,
+    stream_hbm,
     model_ref,
     route_ref,
     res_ref,
     normed_ref,
     routes_ref,
+    q_ref,
+    k_ref,
+    v_ref,
+    stream_ref,
     state,
     mixed,
     normed_heads,
@@ -359,6 +363,8 @@
     h = lax.axis_index("head")
     tokens = q_ref.shape[0]
     rows, width = stream_ref.shape
+    bits = [2**i for i in range(1, seqs.bit_length() - 1)]
+    orders = [bits, bits[::-1]]
     local = q_ref.shape[1] // HD
     block = w_hbm.shape[1]
     part = block // halves
@@ -395,11 +401,22 @@
     def w_at(slot, half):
         return wbuf.at[slot, :, pl.ds(half * part, part)]
 
-    def w_direct(slot, half, peer):
-        return remote(
-            w_hbm.at[:, pl.ds(half * part, part)], w_at(slot, half),
-            wds.at[peer, half], wdr.at[slot, half], peer, h,
-        )
+    def w_first(half, bit):
+        return remote(
+            w_hbm.at[:, pl.ds(half * part, part)], w_at(s, half),
+            wds.at[s, half, bits.index(bit)], wdr.at[s, half], flip(bit), h,
+        )
+
+    def w_relay(slot, half, bit):
+        return remote(
+            w_at(slot, half), w_at(slot, half),
+            wds.at[slot, half, bits.index(bit)], wdr.at[slot, half], flip(bit), h,
+        )
+
+    def later_bits(d, half):
+        order = orders[half]
+        last = max(order.index(bit) for bit in bits if d & bit)
+        return order[last + 1 :]
 
     def w_pass(slot, half):
         return remote(
@@ -423,8 +440,18 @@
         pl.semaphore_signal(barrier, inc=1, device_id=(flip(d), h), device_id_type=MESH)
     for d in range(1, heads):
         pl.semaphore_signal(barrier, inc=1, device_id=(s, line(d)), device_id_type=MESH)
+    loads = [
+        pltpu.make_async_copy(source, target, lsem.at[1 + i])
+        for i, (source, target) in enumerate(
+            [(k_hbm, k_ref), (v_hbm, v_ref), (q_hbm, q_ref), (stream_hbm, stream_ref)]
+        )
+    ]
+    for load in loads:
+        load.start()
     w_own().start()
     routes[h] = route_ref[...]
+    loads[0].wait()
+    loads[1].wait()
 
     def lanes(i):
         return pl.ds(pl.multiple_of(i * HD, HD), HD)
@@ -444,10 +471,12 @@
     state_pass(s).start()
     for d in range(1, heads):
         route_copy(h, line(d)).start()
+    for i in range(len(bits)):
+        for half in range(halves):
+            w_first(half, orders[half][i]).start()
     for half in range(halves):
         w_own_pass(half).start()
-        for d in range(2, seqs, 2):
-            w_direct(s, half, flip(d)).start()
+    loads[2].wait()
 
     row = lax.broadcasted_iota(jnp.int32, (tokens, tokens), 0)
     col = lax.broadcasted_iota(jnp.int32, (tokens, tokens), 1)
@@ -514,12 +543,24 @@
             sum_copy(slot, half, d).start()
 
     w_own().wait()
-    for half in range(halves):
-        for d in range(0, seqs, 2):
+    evens = list(range(0, seqs, 2))
+    schedule = []
+    for low, high in zip(
+        sorted(evens, key=lambda d: (d.bit_count(), d)),
+        sorted(evens, key=lambda d: (d.bit_count(), -d)),
+    ):
+        schedule += [(low, 0), (high, 1)]
+    for i in range(0, len(schedule), 2):
+        pair = schedule[i : i + 2]
+        for d, half in pair:
             if d:
-                w_direct(flip(d), half, flip(d)).wait_recv()
+                w_relay(flip(d), half, bits[0]).wait_recv()
+                for bit in later_bits(d, half):
+                    w_relay(flip(d), half, bit).start()
                 w_pass(flip(d), half).start()
+        for d, half in pair:
             project(flip(d), half)
+        for d, half in pair:
             w_pass(flip(d + 1), half).wait_recv()
             project(flip(d + 1), half)
 
@@ -534,6 +575,7 @@
         route_copy(line(d), line(d)).wait_recv()
     routes_ref[...] = routes[...]
 
+    loads[3].wait()
     group = 16
 
     def normalise(i, carry):
@@ -555,7 +597,11 @@
     for d in range(2, seqs, 2):
         state_direct(s, flip(d)).wait_send()
         for half in range(halves):
-            w_direct(s, half, flip(d)).wait_send()
+            for bit in later_bits(d, half):
+                w_relay(flip(d), half, bit).wait_send()
+    for half in range(halves):
+        for bit in bits:
+            w_first(half, bit).wait_send()
     for d in range(0, seqs, 2):
         state_pass(flip(d)).wait_send()
         for half in range(halves):
@@ -592,9 +638,13 @@
             jax.ShapeDtypeStruct((rows, width), bf),
             jax.ShapeDtypeStruct((heads,) + route.shape, f32),
         ),
-        in_specs=[vmem] * 4 + [anywhere] + [vmem] * 3,
+        in_specs=[anywhere] * 3 + [vmem] + [anywhere] * 2 + [vmem] * 2,
         out_specs=(vmem,) * 3,
         scratch_shapes=[
+            pltpu.VMEM((tokens, features), bf),
+            pltpu.VMEM((tokens, features), bf),
+            pltpu.VMEM((tokens, features), bf),
+            pltpu.VMEM((rows, width), bf),
             pltpu.VMEM((seqs, local, HD, HD), bf),
             pltpu.VMEM((tokens, features), f32),
             pltpu.VMEM((tokens, features), bf),
@@ -607,7 +657,7 @@
             dma((seqs,)),
             dma((seqs,)),
             dma((seqs,)),
-            dma((seqs, halves)),
+            dma((seqs, halves, seqs.bit_length())),
             dma((seqs, halves)),
             dma((seqs, halves)),
             dma((seqs, halves)),
@@ -615,10 +665,10 @@
             dma((seqs, halves, heads)),
             dma((heads,)),
             dma((heads,)),
-            dma((1,)),
+            dma((5,)),
         ],
         compiler_params=pltpu.CompilerParams(
-            collective_id=1, has_side_effects=True, vmem_limit_bytes=50000 * 1024
+            collective_id=1, has_side_effects=True, vmem_limit_bytes=60 * 1024 * 1024
         ),
     )(
         query, key, value, gain.reshape(1, -1), weight, stream, model_gain.reshape(1, -1), route

time: 266 us -> 247 us (0.929)
  Pallas kernels: 251 us -> 239 us
  local copies, waits for them, and re-layouts: 11.2 us -> 4.39 us
    pallas_call x1, Pallas kernels: 175 us -> 166 us  [experts_call(): pl.pallas_call(functools.partial(expert_kernel, seqs, heads, chunks), out...]
    unnamed x19 -> x1, local copies, waits for them, and re-layouts: 10.2 us -> 1.87 us
    pallas_call x1, Pallas kernels: 76 us -> 73.1 us  [attention_call(): pl.pallas_call(functools.partial(attention_kernel, seqs, heads, halves),...]
where the time goes in v3:
time: 247 us
  Pallas kernels  239 us (97%)
  local copies, waits for them, and re-layouts  4.39 us (2%)
  other arithmetic  3.34 us (1%)
    pallas_call x1, Pallas kernels, experts_call(): pl.pallas_call(functools.partial(expert_kernel, seqs, heads, chunks), out...  166 us
    pallas_call x1, Pallas kernels, attention_call(): pl.pallas_call(functools.partial(attention_kernel, seqs, heads, halves),...  73.1 us

profile of v3, /device:TPU:25, one launch (start us, length us, event | category | flops | bytes accessed | tf_op | source)
XLA Modules:
  0.0 246.7 jit_solution(3969107606946647560)
XLA Ops:
  0.0 0.7 convert_element_type.19
  0.7 0.7 pad_maximum_fusion
  1.4 0.7 copy.30.route_ref
  2.1 73.1 %shard_map.127 = (bf16[64,4096]{1,0:T(8,128)(2,1)}, bf16[64,4096]{1,0:T(8,128)(2,1)}, f32[4,64,16]{2,1,0:T(8,128)}) custom-call(bf16[256,1024]{1,0:T(8,128)(2,1)} %q_hbm.1, bf16[256,1024]{1,0:T(8,128)(2,1)} %k_hbm.1, bf16[256,1024]{1,0:T(8,128)(2,1)} %v_hbm.1, f32[1,1024]{1,0:T(1,128)} %bitcast.20, bf16[1024,512]{1,0:T(8,128)(2,1)} %w_hbm.1, ...), custom_call_target="tpu_custom_call" | custom-call | tf_op jit(solution)/shard_map/pallas_call | solution.py:634
  75.2 1.1 fusion.8
  76.3 0.1 copy.31
  76.3 0.1 copy.33
  76.4 0.1 fusion.3
  76.6 0.2 copy.34
  76.7 0.1 compare_reduce_fusion
  76.8 0.1 convolution_select_fusion
  77.0 0.1 eq.62
  77.1 0.3 copy.32
  77.3 0.1 eq.59
  77.4 0.8 select_convert_fusion.mix_ref
  78.3 0.9 fusion.pick_ref
  79.2 165.6 %shard_map.128 = bf16[64,4096]{1,0:T(8,128)(2,1)} custom-call(f32[1,3]{1,0:T(1,128)} %scale_ref.1, bf16[64,4096]{1,0:T(8,128)(2,1)} %get-tuple-element.8.x_ref, bf16[64,4096]{1,0:T(8,128)(2,1)} %get-tuple-element.9.res_ref, bf16[768,256]{1,0:T(8,128)(2,1)} %fusion.pick_ref, bf16[256,768]{1,0:T(8,128)(2,1)} %select_convert_fusion.mix_ref, ...), custom_call_target="tpu_custom_call" | custom-call | tf_op jit(solution)/shard_map/pallas_call | solution.py:285
  244.8 1.9 copy.36
  (3 shorter events, 0.0 us)

commit v4 on v3

--- a/solution.py
+++ b/solution.py
@@ -277,7 +277,7 @@
     rows, width = normed.shape
     hidden = gate.shape[2]
     slots = pick.shape[0] // seqs
-    chunks = 8
+    chunks = 16
     vmem = pl.BlockSpec(memory_space=pltpu.VMEM)
     anywhere = pl.BlockSpec(memory_space=pl.ANY)
     bf, f32 = jnp.bfloat16, jnp.float32

time: 247 us -> 247 us (level)
  no operation moved by 1% of the time
where the time goes in v4:
time: 247 us; the launch traced here: 244 us
  Pallas kernels  237 us (96%)
  local copies, waits for them, and re-layouts  4.39 us (2%)
  other arithmetic  3.34 us (1%)
    pallas_call x1, Pallas kernels, experts_call(): pl.pallas_call(functools.partial(expert_kernel, seqs, heads, chunks), out...  163 us
    pallas_call x1, Pallas kernels, attention_call(): pl.pallas_call(functools.partial(attention_kernel, seqs, heads, halves),...  73.1 us

profile of v4, /device:TPU:25, one launch (start us, length us, event | category | flops | bytes accessed | tf_op | source)
XLA Modules:
  0.0 244.5 jit_solution(2929850301726305229)
XLA Ops:
  0.0 0.7 convert_element_type.19
  0.7 0.7 pad_maximum_fusion
  1.4 0.7 copy.30.route_ref
  2.1 73.1 %shard_map.127 = (bf16[64,4096]{1,0:T(8,128)(2,1)}, bf16[64,4096]{1,0:T(8,128)(2,1)}, f32[4,64,16]{2,1,0:T(8,128)}) custom-call(bf16[256,1024]{1,0:T(8,128)(2,1)} %q_hbm.1, bf16[256,1024]{1,0:T(8,128)(2,1)} %k_hbm.1, bf16[256,1024]{1,0:T(8,128)(2,1)} %v_hbm.1, f32[1,1024]{1,0:T(1,128)} %bitcast.20, bf16[1024,512]{1,0:T(8,128)(2,1)} %w_hbm.1, ...), custom_call_target="tpu_custom_call" | custom-call | tf_op jit(solution)/shard_map/pallas_call | solution.py:634
  75.2 1.1 fusion.8
  76.3 0.1 copy.31
  76.3 0.1 copy.33
  76.4 0.1 fusion.3
  76.6 0.2 copy.34
  76.7 0.1 compare_reduce_fusion
  76.8 0.1 convolution_select_fusion
  77.0 0.1 eq.62
  77.1 0.3 copy.32
  77.3 0.1 eq.59
  77.4 0.8 select_convert_fusion.mix_ref
  78.3 0.9 fusion.pick_ref
  79.2 163.4 %shard_map.128 = bf16[64,4096]{1,0:T(8,128)(2,1)} custom-call(f32[1,3]{1,0:T(1,128)} %scale_ref.1, bf16[64,4096]{1,0:T(8,128)(2,1)} %get-tuple-element.8.x_ref, bf16[64,4096]{1,0:T(8,128)(2,1)} %get-tuple-element.9.res_ref, bf16[768,256]{1,0:T(8,128)(2,1)} %fusion.pick_ref, bf16[256,768]{1,0:T(8,128)(2,1)} %select_convert_fusion.mix_ref, ...), custom_call_target="tpu_custom_call" | custom-call | tf_op jit(solution)/shard_map/pallas_call | solution.py:285
  242.6 1.9 copy.36
  (3 shorter events, 0.0 us)
